TPU v7x, 512 devices: a whole 4x4x16 slice. The times are simulated.
512 devices in a mesh: buyers: 32 (over y, z_lo), goods: 16 (over x, z_hi, core).
Axes of the slice: x: 4, y: 4, z: 16 (z_hi: 2, z_lo: 8; z = z_hi * 8 + z_lo), core: 2. Of those that a mesh axis runs over, the one named last changes fastest.
Arguments:
- buyer_hidden: bfloat16 [40960, 1024], P('buyers', 'goods'), may hold values from -6 to 6
- goods_hidden: bfloat16 [32768, 1024], P('goods', 'buyers'), may hold values from -6 to 6
- buyer_proj: bfloat16 [1024, 128], replicated, may hold values from -0.1875 to 0.1875
- goods_proj: bfloat16 [1024, 128], replicated, may hold values from -0.1875 to 0.1875
- endowment: float32 [40960], P('buyers'), may hold values from 0.5 to 4
Outputs:
- prices: float32 [32768], P('goods')
- utility: float32 [40960], P('buyers')
All inputs are finite; a program needn't handle non-finite values.
Results may differ from a plain program's by a relative error of at most 0.0003.
The roundings to bfloat16 on the way count: a program that leaves them out, or rounds other values in their place, can miss the bound.
Values may be sent and summed in bfloat16 or wider, within the bound.
No kernel may reach another device: no remote copies, remote signals or barrier semaphores. Data moves between devices by JAX's collectives and lax.ppermute only.
A program may use at most 64 MiB of HBM per device.

v0:
```python
import jax
import jax.numpy as jnp
from jax import lax
from jax.sharding import PartitionSpec as P

E = 128
ITERS = 3


def per_device(buyer_hidden, goods_hidden, buyer_proj, goods_proj, endowment):
    proj_rows = buyer_proj
    buyer_sum = jnp.dot(
        lax.all_gather(buyer_hidden, "goods", axis=1, tiled=True),
        proj_rows,
        preferred_element_type=jnp.float32,
    )
    proj_rows = goods_proj
    goods_sum = jnp.dot(
        lax.all_gather(goods_hidden, "buyers", axis=1, tiled=True),
        proj_rows,
        preferred_element_type=jnp.float32,
    )
    buyer_emb = buyer_sum.astype(jnp.bfloat16)
    goods_emb = goods_sum.astype(jnp.bfloat16)
    scores = lax.dot_general(
        buyer_emb, goods_emb, (((1,), (1,)), ((), ())), preferred_element_type=jnp.float32
    )
    values = jax.nn.softplus(scores * E ** (-0.5)).astype(jnp.bfloat16)
    spread = lax.psum(jnp.sum(values, axis=1, dtype=jnp.float32), "goods")
    bid_block = (endowment / spread)[:, None] * values
    prices = spread
    utility = spread
    for repeat in range(ITERS):
        prices = lax.psum(jnp.sum(bid_block, 0), "buyers")
        shares = bid_block / prices[None, :]
        utility = lax.psum(jnp.sum(values * shares, 1), "goods")
        if repeat + 1 < ITERS:
            bid_block = (endowment / utility)[:, None] * values * shares
    return (prices, utility)


def solution(mesh):
    placed = (P("buyers", "goods"), P("goods", "buyers"), P(), P(), P("buyers"))
    return jax.shard_map(
        per_device, mesh=mesh, in_specs=placed, out_specs=(P("goods"), P("buyers")), check_vma=False
    )
```

profile of v0, /device:TPU:1, one launch (start us, length us, event | category | flops | bytes accessed | tf_op | source)
XLA Modules:
  0.0 1007.6 jit_solution(11603073471808425015)
XLA Ops:
  7.2 0.0 copy-start
  7.2 0.0 all-gather.5.cloned.1.call-start
  7.2 0.7 all-gather.5.cloned.1.call-update
  7.9 0.0 all-gather.3.cloned.1.call-start
  8.0 0.7 all-gather.3.cloned.1.call-update
  8.7 223.9 %all-gather.5.cloned.1.call-done = bf16[2048,1024]{0,1:T(8,128)(2,1)} async-done(((bf16[2048,32]{0,1:T(8,128)(2,1)}), bf16[2048,1024]{0,1:T(8,128)(2,1)}) %all-gather.5.cloned.1.call-update) | async-done | bytes 4194320 | tf_op jit(solution)/shard_map/all_gather | solution.py:19
  232.5 3.5 convolution_convert_fusion
  236.1 0.0 copy-start.1
  236.1 117.2 %all-gather.3.cloned.1.call-done = bf16[1280,1024]{0,1:T(8,128)(2,1)} async-done(((bf16[1280,64]{0,1:T(8,128)(2,1)}), bf16[1280,1024]{0,1:T(8,128)(2,1)}) %all-gather.3.cloned.1.call-update) | async-done | bytes 2621456 | tf_op jit(solution)/shard_map/all_gather | solution.py:13
  353.3 0.0 copy-done
  353.3 11.8 %convert_reduce_fusion = (f32[1280]{0:T(1024)S(1)}, bf16[1280,2048]{1,0:T(8,128)(2,1)}) fusion(bf16[2048,128]{1,0:T(8,128)(2,1)S(1)} %convolution_convert_fusion, bf16[1280,1024]{0,1:T(8,128)(2,1)} %all-gather.3.cloned.1.call-done, bf16[1024,128]{1,0:T(8,128)(2,1)S(1)} %copy-done), kind=kOutput, calls=%fused_computation.7 | convolution fusion | flops 1033009920 | bytes 8655872 | tf_op jit(solution)/shard_map/dot_general | solution.py:25
  365.2 62.1 %psum.49 = f32[1280]{0:T(1024)S(1)} all-reduce(f32[1280]{0:T(1024)S(1)} %get-tuple-element.2), channel_id=1, replica_groups=mesh['buyers'=32,'goods'=16] {'goods'}, use_global_device_ids=true, to_apply=%region_1.2 | all-reduce | flops 1280 | bytes 10240 | tf_op jit(solution)/shard_map/psum | solution.py:29
  427.3 0.0 copy-done.1
  427.3 3.6 fusion.1
  430.9 101.5 %psum.50 = f32[2048]{0:T(1024)S(1)} all-reduce(f32[2048]{0:T(1024)S(1)} %fusion.1), channel_id=1, replica_groups=mesh['buyers'=32,'goods'=16] {'buyers'}, use_global_device_ids=true, to_apply=%region_3.4 | all-reduce | flops 2048 | bytes 16384 | tf_op jit(solution)/shard_map/psum | solution.py:34
  532.3 4.4 fusion.2
  536.7 84.0 %psum.51 = f32[1280]{0:T(1024)S(1)} all-reduce(f32[1280]{0:T(1024)S(1)} %fusion.2), channel_id=1, replica_groups=mesh['buyers'=32,'goods'=16] {'goods'}, use_global_device_ids=true, to_apply=%region_5.6 | all-reduce | flops 1280 | bytes 10240 | tf_op jit(solution)/shard_map/psum | solution.py:36
  620.7 4.7 fusion.9
  625.5 101.0 %psum.52 = f32[2048]{0:T(1024)S(1)} all-reduce(f32[2048]{0:T(1024)S(1)} %fusion.9), channel_id=1, replica_groups=mesh['buyers'=32,'goods'=16] {'buyers'}, use_global_device_ids=true, to_apply=%region_7.8 | all-reduce | flops 2048 | bytes 16384 | tf_op jit(solution)/shard_map/psum | solution.py:34
  726.5 4.9 fusion.4
  731.4 76.3 %psum.53 = f32[1280]{0:T(1024)S(1)} all-reduce(f32[1280]{0:T(1024)S(1)} %fusion.4), channel_id=1, replica_groups=mesh['buyers'=32,'goods'=16] {'goods'}, use_global_device_ids=true, to_apply=%region_9.10 | all-reduce | flops 1280 | bytes 10240 | tf_op jit(solution)/shard_map/psum | solution.py:36
  807.7 6.5 fusion.8
  814.2 102.8 %psum.54 = f32[2048]{0:T(1024)S(1)} all-reduce(f32[2048]{0:T(1024)S(1)} %fusion.8), channel_id=1, replica_groups=mesh['buyers'=32,'goods'=16] {'buyers'}, use_global_device_ids=true, to_apply=%region_11.12 | all-reduce | flops 2048 | bytes 16384 | tf_op jit(solution)/shard_map/psum | solution.py:34
  917.0 0.0 copy-start.2
  917.0 6.5 fusion.6
  923.5 77.4 %psum.55 = f32[1280]{0:T(1024)} all-reduce(f32[1280]{0:T(1024)S(1)} %fusion.6), channel_id=1, replica_groups=mesh['buyers'=32,'goods'=16] {'goods'}, use_global_device_ids=true, to_apply=%region_13.14 | all-reduce | flops 1280 | bytes 10240 | tf_op jit(solution)/shard_map/psum | solution.py:36
  1000.8 0.0 copy-done.2
  (3 shorter events, 0.0 us)
Async XLA Ops:
  7.2 346.2 %copy-start = (bf16[1024,128]{1,0:T(8,128)(2,1)S(1)}, bf16[1024,128]{1,0:T(8,128)(2,1)}, u32[]{:S(2)}) copy-start(bf16[1024,128]{1,0:T(8,128)(2,1)} %param.7) | copy-start | bytes 786436
  7.2 225.4 %all-gather.5.cloned.1.call-start = ((), (), s32[]{:S(2)}) async-start(), calls=%async_computation.1 | async-start | bytes 4325376 | tf_op jit(solution)/shard_map/all_gather | solution.py:19
  7.9 345.4 %all-gather.3.cloned.1.call-start = ((), (), s32[]{:S(2)}) async-start(), calls=%async_computation | async-start | bytes 2785280 | tf_op jit(solution)/shard_map/all_gather | solution.py:13
  236.1 191.2 %copy-start.1 = (f32[1280]{0:T(1024)S(1)}, f32[1280]{0:T(1024)}, u32[]{:S(2)}) copy-start(f32[1280]{0:T(1024)} %param.9) | copy-start | bytes 15364
  917.0 83.8 %copy-start.2 = (f32[2048]{0:T(1024)}, f32[2048]{0:T(1024)S(1)}, u32[]{:S(2)}) copy-start(f32[2048]{0:T(1024)S(1)} %psum.54) | copy-start | bytes 24580
Sparse Core Ops, SparseCore 0:
  10.1 222.4 all-gather.4
  235.8 117.4 all-gather.2
where the time goes:
time: 1010 us
  blocking collectives  605 us (60%)
  waiting for transfers between devices  343 us (34%)
  other arithmetic  30.6 us (3%)
  matrix products  15.3 us (2%)
  between operations  14.2 us (1%)
    psum x3, blocking collectives, per_device(): prices = lax.psum(jnp.sum(bid_block, 0), 'buyers')  305 us
    psum x3, blocking collectives, per_device(): utility = lax.psum(jnp.sum(values * shares, 1), 'goods')  238 us
    all_gather x1, waiting for transfers between devices, per_device(): lax.all_gather(goods_hidden, 'buyers', axis=1, tiled=True)  224 us
    all_gather x1, waiting for transfers between devices, per_device(): lax.all_gather(buyer_hidden, 'goods', axis=1, tiled=True)  117 us
    psum x1, blocking collectives, per_device(): spread = lax.psum(jnp.sum(values, axis=1, dtype=jnp.float32), 'goods')  62.1 us
  transfers between devices with their start and end apart: 2, of which 2 were waited for; matrix products, arithmetic and copies ran while one was open for 0% of the time, Pallas kernels for 0%

commit v1 on v0

--- a/solution.py
+++ b/solution.py
@@ -10,7 +10,10 @@
 def per_device(buyer_hidden, goods_hidden, buyer_proj, goods_proj, endowment):
     proj_rows = buyer_proj
     buyer_sum = jnp.dot(
-        lax.all_gather(buyer_hidden, "goods", axis=1, tiled=True),
+        jnp.concatenate(
+            lax.all_to_all(jnp.stack([buyer_hidden] * lax.axis_size("goods")), "goods", 0, 0),
+            axis=1,
+        ),
         proj_rows,
         preferred_element_type=jnp.float32,
     )

time: 1010 us -> 966 us (0.956)
  waiting for transfers between devices: 343 us -> 266 us
  starting transfers between devices: 0.08 us -> 19.1 us
  blocking collectives: 605 us -> 617 us
    all_gather x1 -> x0, waiting for transfers between devices: 117 us -> none  [per_device(): lax.all_gather(buyer_hidden, 'goods', axis=1, tiled=True)]
    all_gather x1, waiting for transfers between devices: 224 us -> 266 us  [per_device(): lax.all_gather(goods_hidden, 'buyers', axis=1, tiled=True)]
    all_to_all x0 -> x1, starting transfers between devices: none -> 19.1 us  [per_device(): lax.all_to_all(jnp.stack([buyer_hidden] * lax.axis_size('goods')), 'goods...]
    psum x1, blocking collectives: 62.1 us -> 76.7 us  [per_device(): spread = lax.psum(jnp.sum(values, axis=1, dtype=jnp.float32), 'goods')]
  transfers between devices with their start and end apart: 2 -> 2, of which waited for: 2 -> 1; matrix products, arithmetic and copies ran while one was open for 0% -> 0% of each run, Pallas kernels for 0% -> 0%
where the time goes in v1:
time: 966 us
  blocking collectives  617 us (64%)
  waiting for transfers between devices  266 us (28%)
  other arithmetic  30.5 us (3%)
  starting transfers between devices  19.1 us (2%)
  matrix products  15.9 us (2%)
  between operations  14.2 us (1%)
    psum x3, blocking collectives, per_device(): prices = lax.psum(jnp.sum(bid_block, 0), 'buyers')  310 us
    all_gather x1, waiting for transfers between devices, per_device(): lax.all_gather(goods_hidden, 'buyers', axis=1, tiled=True)  266 us
    psum x3, blocking collectives, per_device(): utility = lax.psum(jnp.sum(values * shares, 1), 'goods')  230 us
    psum x1, blocking collectives, per_device(): spread = lax.psum(jnp.sum(values, axis=1, dtype=jnp.float32), 'goods')  76.7 us
  transfers between devices with their start and end apart: 2, of which 1 were waited for; matrix products, arithmetic and copies ran while one was open for 0% of the time, Pallas kernels for 0%

profile of v1, /device:TPU:1, one launch (start us, length us, event | category | flops | bytes accessed | tf_op | source)
XLA Modules:
  0.0 965.8 jit_solution(1151589199503480627)
XLA Ops:
  7.2 0.0 copy-start
  7.2 0.0 copy-start.3
  7.2 2.8 stack.2
  9.9 19.1 %all-to-all-start = ((bf16[16,1280,64]{1,2,0:T(8,128)(2,1)}), bf16[16,1280,64]{1,2,0:T(8,128)(2,1)S(1)}, u32[]{:S(2)}, u32[]{:S(2)}) async-start(bf16[16,1280,64]{1,2,0:T(8,128)(2,1)} %stack.2), calls=%async_computation | async-start | bytes 5242880 | tf_op jit(solution)/shard_map/all_to_all | solution.py:14
  29.0 0.0 all-gather.2.cloned.1.call-start
  29.0 0.7 all-gather.2.cloned.1.call-update
  29.7 265.8 %all-gather.2.cloned.1.call-done = bf16[2048,1024]{0,1:T(8,128)(2,1)} async-done(((bf16[2048,32]{0,1:T(8,128)(2,1)}), bf16[2048,1024]{0,1:T(8,128)(2,1)}) %all-gather.2.cloned.1.call-update) | async-done | bytes 4194320 | tf_op jit(solution)/shard_map/all_gather | solution.py:22
  295.5 0.0 copy-done.3
  295.5 4.3 convolution_convert_fusion
  299.8 0.0 all-to-all-done
  299.8 0.0 copy-done
  299.8 0.0 copy-start.1
  299.9 11.6 %convert_reduce_fusion = (f32[1280]{0:T(1024)S(1)}, bf16[1280,2048]{1,0:T(8,128)(2,1)}) fusion(bf16[2048,128]{1,0:T(8,128)(2,1)} %convolution_convert_fusion, bf16[1280,1024]{0,1:T(8,128)(2,1)S(1)} %bitcast.8, bf16[1024,128]{1,0:T(8,128)(2,1)S(1)} %copy-done), kind=kOutput, calls=%fused_computation.7 | convolution fusion | flops 1033009920 | bytes 8655872 | tf_op jit(solution)/shard_map/dot_general | solution.py:28
  311.4 76.7 %psum.49 = f32[1280]{0:T(1024)S(1)} all-reduce(f32[1280]{0:T(1024)S(1)} %get-tuple-element.2), channel_id=1, replica_groups=mesh['buyers'=32,'goods'=16] {'goods'}, use_global_device_ids=true, to_apply=%region_1.2 | all-reduce | flops 1280 | bytes 10240 | tf_op jit(solution)/shard_map/psum | solution.py:32
  388.1 0.0 copy-done.1
  388.2 3.6 fusion.1
  391.8 106.0 %psum.50 = f32[2048]{0:T(1024)S(1)} all-reduce(f32[2048]{0:T(1024)S(1)} %fusion.1), channel_id=1, replica_groups=mesh['buyers'=32,'goods'=16] {'buyers'}, use_global_device_ids=true, to_apply=%region_3.4 | all-reduce | flops 2048 | bytes 16384 | tf_op jit(solution)/shard_map/psum | solution.py:37
  497.7 4.4 fusion.2
  502.1 76.9 %psum.51 = f32[1280]{0:T(1024)S(1)} all-reduce(f32[1280]{0:T(1024)S(1)} %fusion.2), channel_id=1, replica_groups=mesh['buyers'=32,'goods'=16] {'goods'}, use_global_device_ids=true, to_apply=%region_5.6 | all-reduce | flops 1280 | bytes 10240 | tf_op jit(solution)/shard_map/psum | solution.py:39
  579.0 4.7 fusion.9
  583.7 101.0 %psum.52 = f32[2048]{0:T(1024)S(1)} all-reduce(f32[2048]{0:T(1024)S(1)} %fusion.9), channel_id=1, replica_groups=mesh['buyers'=32,'goods'=16] {'buyers'}, use_global_device_ids=true, to_apply=%region_7.8 | all-reduce | flops 2048 | bytes 16384 | tf_op jit(solution)/shard_map/psum | solution.py:37
  684.7 4.9 fusion.4
  689.6 76.3 %psum.53 = f32[1280]{0:T(1024)S(1)} all-reduce(f32[1280]{0:T(1024)S(1)} %fusion.4), channel_id=1, replica_groups=mesh['buyers'=32,'goods'=16] {'goods'}, use_global_device_ids=true, to_apply=%region_9.10 | all-reduce | flops 1280 | bytes 10240 | tf_op jit(solution)/shard_map/psum | solution.py:39
  765.9 6.5 fusion.8
  772.4 102.7 %psum.54 = f32[2048]{0:T(1024)S(1)} all-reduce(f32[2048]{0:T(1024)S(1)} %fusion.8), channel_id=1, replica_groups=mesh['buyers'=32,'goods'=16] {'buyers'}, use_global_device_ids=true, to_apply=%region_11.12 | all-reduce | flops 2048 | bytes 16384 | tf_op jit(solution)/shard_map/psum | solution.py:37
  875.2 0.0 copy-start.2
  875.2 6.5 fusion.6
  881.7 77.3 %psum.55 = f32[1280]{0:T(1024)} all-reduce(f32[1280]{0:T(1024)S(1)} %fusion.6), channel_id=1, replica_groups=mesh['buyers'=32,'goods'=16] {'goods'}, use_global_device_ids=true, to_apply=%region_13.14 | all-reduce | flops 1280 | bytes 10240 | tf_op jit(solution)/shard_map/psum | solution.py:39
  959.0 0.0 copy-done.2
  (3 shorter events, 0.0 us)
Async XLA Ops:
  7.2 292.7 %copy-start = (bf16[1024,128]{1,0:T(8,128)(2,1)S(1)}, bf16[1024,128]{1,0:T(8,128)(2,1)}, u32[]{:S(2)}) copy-start(bf16[1024,128]{1,0:T(8,128)(2,1)} %param.7) | copy-start | bytes 786436
  7.2 288.3 %copy-start.3 = (bf16[1024,128]{1,0:T(8,128)(2,1)S(1)}, bf16[1024,128]{1,0:T(8,128)(2,1)}, u32[]{:S(2)}) copy-start(bf16[1024,128]{1,0:T(8,128)(2,1)} %param.8) | copy-start | bytes 786436
  9.9 289.9 %all-to-all-start = ((bf16[16,1280,64]{1,2,0:T(8,128)(2,1)}), bf16[16,1280,64]{1,2,0:T(8,128)(2,1)S(1)}, u32[]{:S(2)}, u32[]{:S(2)}) async-start(bf16[16,1280,64]{1,2,0:T(8,128)(2,1)} %stack.2), calls=%async_computation | async-start | bytes 5242880 | tf_op jit(solution)/shard_map/all_to_all | solution.py:14
  29.0 266.5 %all-gather.2.cloned.1.call-start = ((), (), s32[]{:S(2)}) async-start(), calls=%async_computation.1 | async-start | bytes 4325376 | tf_op jit(solution)/shard_map/all_gather | solution.py:22
  299.8 88.3 %copy-start.1 = (f32[1280]{0:T(1024)S(1)}, f32[1280]{0:T(1024)}, u32[]{:S(2)}) copy-start(f32[1280]{0:T(1024)} %param.9) | copy-start | bytes 15364
  875.2 83.8 %copy-start.2 = (f32[2048]{0:T(1024)}, f32[2048]{0:T(1024)S(1)}, u32[]{:S(2)}) copy-start(f32[2048]{0:T(1024)S(1)} %psum.54) | copy-start | bytes 24580
Sparse Core Ops, SparseCore 0:
  31.9 263.5 all-gather.1
